TPU v7x, 32 devices: a whole 2x2x4 slice. The times are simulated.
32 devices in a mesh: seq: 8 (over z, x), tp: 4 (over y, core).
Axes of the slice: x: 2, y: 2, z: 4, core: 2. Of those that a mesh axis runs over, the one named last changes fastest.
Arguments:
- tokens_in: bfloat16 [4, 16, 1024], replicated, may hold values from -6 to 6
- key_cache: bfloat16 [16, 2048, 1024], P(None, 'seq', 'tp'), may hold values from -6 to 6
- value_cache: bfloat16 [16, 2048, 1024], P(None, 'seq', 'tp'), may hold values from -6 to 6
- cache_len: int32 [16], replicated, may hold values from 1 to 2048, as said below
- bucket_table: int32 [2052], replicated, may hold values from 0 to 31, as said below
- rel_bias: float32 [32, 16], P(None, 'tp'), may hold values from -4 to 283
- attn_gain: float32 [1024], replicated, may hold values from 0.1 to 1.9
- moe_gain: float32 [1024], replicated, may hold values from 0.1 to 1.9
- w_qkv: bfloat16 [3, 1024, 1024], P(None, None, 'tp'), may hold values from -0.1875 to 0.1875
- w_out: bfloat16 [1024, 1024], P('tp'), may hold values from -0.1875 to 0.1875
- router: bfloat16 [1024, 16], replicated, may hold values from -0.1875 to 0.1875
- expert_choice: int32 [4, 16, 2], replicated, may hold values from 0 to 15, all different within a row
- w_gate_up: bfloat16 [2, 45056, 1024], P(None, ('seq', 'tp')), may hold values from -0.1875 to 0.1875
- w_down: bfloat16 [45056, 1024], P(('seq', 'tp')), may hold values from -0.109375 to 0.109375
Outputs:
- layer_out: bfloat16 [4, 16, 1024], replicated
Inputs may be any that keep to these rules, and one draw needn't show every extreme that they name: Request r's cache holds its positions 0 to cache_len[r] - 1; some request holds exactly 2048. `bucket_table`: non-decreasing in the distance, 0 at distance 0. `expert_choice`: the 2 experts of a token differ.
All inputs are finite; a program needn't handle non-finite values.
Results may differ from a plain program's by a relative error of at most 0.012.
Values sent between devices are 32-bit elements; how exact they have to be, the bound alone decides.
No kernel may reach another device: no remote copies, remote signals or barrier semaphores. Data moves between devices by JAX's collectives and lax.ppermute only.
A program may use at most 64 MiB of HBM per device.

v0:
```python
import jax
import jax.numpy as jnp
from jax import lax
from jax.sharding import PartitionSpec as P

HEAD_DIM = 64
FF = 2816
NEG = -1e30
EPS = 1e-06


def rms_scale(values, gain_vec):
    return values * lax.rsqrt(jnp.mean(values * values, axis=-1, keepdims=True) + EPS) * gain_vec


def on_device(
    tokens_in,
    key_cache,
    value_cache,
    cache_len,
    bucket_table,
    rel_bias,
    attn_gain,
    moe_gain,
    w_qkv,
    w_out,
    router,
    expert_choice,
    w_gate_up,
    w_down,
):
    steps_all, requests, model_width = tokens_in.shape
    cache_rows = key_cache.shape[1]
    heads_local = key_cache.shape[2] // HEAD_DIM
    table_len = bucket_table.shape[0]
    num_buckets = rel_bias.shape[0]
    num_experts = router.shape[1]
    hidden_local = w_down.shape[0]
    bucket_ids = jnp.arange(num_buckets, dtype=jnp.int32)

    def bias_lookup(buckets, pattern):
        onehot = (buckets[..., None] == bucket_ids).astype(jnp.float32)
        return jnp.einsum(pattern, onehot, rel_bias, precision=lax.Precision.HIGHEST)

    normed = rms_scale(tokens_in.astype(jnp.float32), attn_gain).astype(jnp.bfloat16)
    projected = jnp.einsum(
        "srd,kdf->ksrf", normed, w_qkv, preferred_element_type=jnp.float32
    ).astype(jnp.bfloat16)
    head_shape = (steps_all, requests, heads_local, HEAD_DIM)
    queries = projected[0].reshape(head_shape)
    fresh_keys = projected[1].reshape(head_shape)
    fresh_values = projected[2].reshape(head_shape)
    keys_heads = key_cache.reshape(requests, cache_rows, heads_local, HEAD_DIM)
    values_heads = value_cache.reshape(requests, cache_rows, heads_local, HEAD_DIM)
    positions = lax.axis_index("seq") * cache_rows + jnp.arange(cache_rows, dtype=jnp.int32)
    live_rows = positions[None, :] < cache_len[:, None]

    def cache_part(query_blk, step_ids, keys_blk, vals_blk, lens_blk, live_blk):
        scores = jnp.einsum(
            "srhd,rchd->srhc", query_blk, keys_blk, preferred_element_type=jnp.float32
        )
        distance = lens_blk[None, :, None] + step_ids[:, None, None] - positions[None, None, :]
        buckets = jnp.take(bucket_table, jnp.clip(distance, 0, table_len - 1))
        scores = scores + bias_lookup(buckets, "srcb,bh->srhc")
        usable = live_blk[None, :, None, :]
        scores = jnp.where(usable, scores, NEG)
        maxima = jnp.max(scores, axis=-1)
        weights = jnp.where(usable, jnp.exp(scores - maxima[..., None]), 0.0)
        summed = jnp.einsum(
            "srhc,rchd->srhd", weights, vals_blk, preferred_element_type=jnp.float32
        )
        return (maxima, jnp.sum(weights, axis=-1), summed)

    def attend_cache(query_blk, step_ids):
        return cache_part(query_blk, step_ids, keys_heads, values_heads, cache_len, live_rows)

    def merge_cache(maxima, totals, summed):
        overall = lax.pmax(maxima, "seq")
        factor = jnp.exp(maxima - overall)
        totals, summed = lax.psum((totals * factor, summed * factor[..., None]), "seq")
        return (overall, totals, summed)

    def attend_recent(query_blk, step_ids):
        scores = jnp.einsum(
            "srhd,jrhd->srhj", query_blk, fresh_keys, preferred_element_type=jnp.float32
        )
        distance = step_ids[:, None] - jnp.arange(steps_all, dtype=jnp.int32)[None, :]
        buckets = jnp.take(bucket_table, jnp.clip(distance, 0, table_len - 1))
        scores = scores + bias_lookup(buckets, "sjb,bh->shj")[:, None]
        usable = (distance >= 0)[:, None, None, :]
        scores = jnp.where(usable, scores, NEG)
        maxima = jnp.max(scores, axis=-1)
        weights = jnp.where(usable, jnp.exp(scores - maxima[..., None]), 0.0)
        summed = jnp.einsum(
            "srhj,jrhd->srhd", weights, fresh_values, preferred_element_type=jnp.float32
        )
        return (maxima, jnp.sum(weights, axis=-1), summed)

    first_col = (lax.axis_index("seq") * lax.axis_size("tp") + lax.axis_index("tp")) * hidden_local
    col_expert = (first_col + jnp.arange(hidden_local, dtype=jnp.int32)) // FF
    owner = (col_expert[None, :] == jnp.arange(num_experts, dtype=jnp.int32)[:, None]).astype(
        jnp.float32
    )

    def layer(start, step_count):
        step_ids = jnp.arange(start, start + step_count, dtype=jnp.int32)
        query_blk = queries[start : start + step_count]
        cache_max, cache_tot, cache_sum = merge_cache(*attend_cache(query_blk, step_ids))
        new_max, new_tot, new_sum = attend_recent(query_blk, step_ids)
        joint = jnp.maximum(cache_max, new_max)
        scale_cache = jnp.exp(cache_max - joint)
        scale_new = jnp.exp(new_max - joint)
        totals = cache_tot * scale_cache + new_tot * scale_new
        summed = cache_sum * scale_cache[..., None] + new_sum * scale_new[..., None]
        attended = (
            (summed / totals[..., None])
            .reshape(step_count, requests, heads_local * HEAD_DIM)
            .astype(jnp.bfloat16)
        )
        partial_value = jnp.einsum(
            "srf,fd->srd", attended, w_out, preferred_element_type=jnp.float32
        )
        mid = tokens_in[start : start + step_count].astype(jnp.float32) + lax.psum(
            partial_value, "tp"
        )
        moe_in = rms_scale(mid, moe_gain).astype(jnp.bfloat16)
        logits = jnp.einsum("srd,de->sre", moe_in, router, preferred_element_type=jnp.float32)
        picked = expert_choice[start : start + step_count][..., None] == jnp.arange(
            num_experts, dtype=jnp.int32
        )
        chosen = jnp.sum(jnp.where(picked, logits[:, :, None, :], 0.0), axis=-1)
        leading = jax.nn.sigmoid(chosen[..., 0] - chosen[..., 1])
        gate_pair = jnp.stack([leading, 1.0 - leading], axis=-1)
        per_expert = jnp.sum(jnp.where(picked, gate_pair[..., None], 0.0), axis=2)
        coef = jnp.einsum("sre,ef->srf", per_expert, owner, precision=lax.Precision.HIGHEST)
        gate_up = jnp.einsum("srd,kfd->ksrf", moe_in, w_gate_up, preferred_element_type=jnp.float32)
        hidden = (jax.nn.gelu(gate_up[0], approximate=True) * gate_up[1] * coef).astype(
            jnp.bfloat16
        )
        expert_part = jnp.einsum("srf,fd->srd", hidden, w_down, preferred_element_type=jnp.float32)
        mixture = lax.psum(expert_part, ("seq", "tp"))
        return (mid + mixture).astype(jnp.bfloat16)

    outputs = [layer(start, 1) for start in range(steps_all)]
    return jnp.concatenate(outputs, axis=0)


def solution(mesh):
    return jax.shard_map(
        on_device,
        mesh=mesh,
        in_specs=(
            P(),
            P(None, "seq", "tp"),
            P(None, "seq", "tp"),
            P(),
            P(),
            P(None, "tp"),
            P(),
            P(),
            P(None, None, "tp"),
            P("tp", None),
            P(),
            P(),
            P(None, ("seq", "tp"), None),
            P(("seq", "tp"), None),
        ),
        out_specs=P(),
        check_vma=False,
    )
```

profile of v0, /device:TPU:0, one launch (start us, length us, event | category | flops | bytes accessed | tf_op | source)
XLA Modules:
  0.0 458.9 jit_solution(6743066980730547285)
XLA Ops:
  9.3 23.0 %gather_fusion.4 = s32[4096]{0:T(1024)S(1)} fusion(s32[2052]{0:T(1024)S(1)} %copy-done.1, s32[4096]{0:T(1024)S(1)} %broadcast_clamp_fusion.1), kind=kCustom, calls=%fused_computation.3.clone | custom fusion | bytes 49152 | tf_op jit(solution)/shard_map/jit(_take)/gather | solution.py:63
  32.4 23.0 %gather_fusion.6 = s32[4096]{0:T(1024)S(1)} fusion(s32[2052]{0:T(1024)S(1)} %copy-done.1, s32[4096]{0:T(1024)S(1)} %broadcast_clamp_fusion), kind=kCustom, calls=%fused_computation.4.clone | custom fusion | bytes 49152 | tf_op jit(solution)/shard_map/jit(_take)/gather | solution.py:63
  55.5 23.0 %gather_fusion.2 = s32[4096]{0:T(1024)S(1)} fusion(s32[2052]{0:T(1024)S(1)} %copy-done.1, s32[4096]{0:T(1024)S(1)} %broadcast_clamp_fusion.2), kind=kCustom, calls=%fused_computation.2.clone | custom fusion | bytes 49152 | tf_op jit(solution)/shard_map/jit(_take)/gather | solution.py:63
  79.3 23.0 %gather_fusion = s32[4096]{0:T(1024)S(1)} fusion(s32[2052]{0:T(1024)S(1)} %copy-done.1, s32[4096]{0:T(1024)S(1)} %broadcast_clamp_fusion.3), kind=kCustom, calls=%fused_computation.clone | custom fusion | bytes 49152 | tf_op jit(solution)/shard_map/jit(_take)/gather | solution.py:63
  103.0 1.8 fusion.9
  105.2 3.9 copy.134
  109.2 2.0 fusion.206
  112.2 2.0 fusion.205
  115.2 2.8 fusion.204
  126.0 23.4 %all-reduce.2 = (f32[1,16,4]{1,2,0:T(4,128)S(1)}, f32[1,16,4]{1,2,0:T(4,128)S(1)}, f32[1,16,4]{1,2,0:T(4,128)S(1)}, f32[1,16,4]{1,2,0:T(4,128)S(1)}) all-reduce(f32[1,16,4]{1,2,0:T(4,128)} %bitcast.599, f32[1,16,4]{1,2,0:T(4,128)} %bitcast.601, f32[1,16,4]{1,2,0:T(4,128)} %bitcast.598, ...), channel_id=1, replica_groups=mesh['seq'=8,'tp'=4] {'seq'}, use_global_device_ids=true, to_apply=%region_2.4 | all-reduce | flops 256 | bytes 2048 | tf_op jit(solution)/shard_map/pmax | solution.py:78
  151.0 1.3 bitcast_multiply_fusion.5
  152.4 3.9 copy.135
  156.4 2.4 fusion.63
  176.6 1.5 convolution_bitcast_fusion.15
  178.1 1.3 copy.160
  179.4 1.4 copy.186
  182.2 1.4 fusion.194
  183.6 1.4 copy.193
  185.8 1.4 fusion.193
  187.2 1.4 fusion.196
  189.8 1.3 gather_fusion.1
  191.8 1.4 convolution_bitcast_fusion.18
  193.3 1.4 copy.138
  195.9 1.3 gather_fusion.3
  199.5 1.5 reshape_squeeze.8
  202.6 1.4 fusion.192
  203.9 1.4 copy.180
  205.3 1.4 copy.187
  206.7 1.7 fusion.108
  208.4 1.7 fusion.106
  210.0 1.4 copy.171
  212.8 1.4 fusion.190
  214.2 1.4 copy.173
  215.6 1.7 fusion.110
  217.3 1.4 copy.194
  218.7 1.7 fusion.104
  220.3 1.4 fusion.189
  221.7 10.9 %all-reduce.10.cloned.1.call-done = (f32[1,16,4,64]{3,2,1,0:T(4,128)}, f32[1,16,4]{1,2,0:T(4,128)}, f32[1,16,4,64]{3,2,1,0:T(4,128)}, f32[1,16,4]{1,2,0:T(4,128)...) async-done(((f32[1,16,4,64]{3,2,1,0:T(4,128)}, f32[1,16,4]{1,2,0:T(4,128)}, f32[1,16,4,64]{3,2,1,0:T(4,128)}, ...) | async-done | bytes 66576 | tf_op jit(solution)/shard_map/psum | solution.py:80
  234.7 1.3 fusion.178
  236.0 1.3 copy.161
  239.3 1.3 fusion.184
  240.6 1.4 copy.139
  241.9 1.3 copy.157
  243.3 1.3 copy.155
  244.6 1.5 fusion.102
  246.9 1.3 copy.164
  248.2 1.3 copy.162
  249.6 1.5 fusion.103
  251.1 1.4 convert_element_type.133
  252.5 1.3 copy.150
  253.8 1.3 copy.148
  255.2 1.5 fusion.101
  256.7 1.4 convert_element_type.121
  259.4 1.5 fusion.100
  260.9 1.4 convert_element_type.115
  262.4 1.5 convolution_bitcast_fusion.14
  263.9 1.5 convolution_bitcast_fusion.13
  265.4 1.5 convolution_bitcast_fusion.11
  268.7 30.7 %all-reduce.12.cloned.1.call-done = (f32[1,16,1024]{2,1,0:T(8,128)}, f32[1,16,1024]{2,1,0:T(8,128)}, f32[1,16,1024]{2,1,0:T(8,128)}, f32[1,16,1024]{2,1,0:T(8,128)}) async-done(((f32[1,16,1024]{2,1,0:T(8,128)}, f32[1,16,1024]{2,1,0:T(8,128)}, f32[1,16,1024]{2,1,0:T(8,128)}, f32[1,16,1024]{2,1,0:T(8,128)}), (f32[1,16,1024]{2,1,0:T(8,128)}, f32[1,16,1024]{2,1,0:T(8,128)}, f32[1,16,1024]{2,1,0:T(8,128)}, ...) | async-done | bytes 262160 | tf_op jit(solution)/shard_map/psum | solution.py:123
  303.4 4.4 fusion.95
  307.8 4.4 convolution_bitcast_fusion
  312.3 4.2 convolution_bitcast_fusion.1
  316.7 1.6 convolution_bitcast_fusion.2
  324.6 126.1 %all-reduce.8.cloned.1.call-done = (f32[1,16,1024]{2,1,0:T(8,128)}, f32[1,16,1024]{2,1,0:T(8,128)}, f32[1,16,1024]{2,1,0:T(8,128)}, f32[1,16,1024]{2,1,0:T(8,128)}) async-done(((f32[1,16,1024]{2,1,0:T(8,128)}, f32[1,16,1024]{2,1,0:T(8,128)}, f32[1,16,1024]{2,1,0:T(8,128)}, f32[1,16,1024]{2,1,0:T(8,128)}), (f32[1,16,1024]{2,1,0:T(8,128)}, f32[1,16,1024]{2,1,0:T(8,128)}, f32[1,16,1024]{2,1,0:T(8,128)}, ...) | async-done | bytes 262160 | tf_op jit(solution)/shard_map/psum | solution.py:141
  (196 shorter events, 64.6 us)
Async XLA Ops:
  6.5 313.0 %copy-start = (bf16[1408,1024]{1,0:T(8,128)(2,1)S(1)}, bf16[1408,1024]{1,0:T(8,128)(2,1)}, u32[]{:S(2)}) copy-start(bf16[1408,1024]{1,0:T(8,128)(2,1)} %param.31) | copy-start | bytes 8650756
  6.5 2.8 copy-start.1
  6.5 226.1 %all-reduce.10.cloned.1.call-start = ((), (), s32[]{:S(2)}) async-start(), calls=%async_computation.1 | async-start | bytes 278528 | tf_op jit(solution)/shard_map/psum | solution.py:80
  55.5 23.1 %copy-start.20 = (s32[16]{0:T(128)S(1)}, s32[16]{0:T(128)}, u32[]{:S(2)}) copy-start(s32[16]{0:T(128)} %param.21) | copy-start | bytes 196
  79.3 23.8 %copy-start.4 = (bf16[4,16,1024]{2,1,0:T(8,128)(2,1)S(1)}, bf16[4,16,1024]{2,1,0:T(8,128)(2,1)}, u32[]{:S(2)}) copy-start(bf16[4,16,1024]{2,1,0:T(8,128)(2,1)} %param.18) | copy-start | bytes 393220
  79.3 23.8 %copy-start.18 = (f32[1024]{0:T(1024)S(1)}, f32[1024]{0:T(1024)}, u32[]{:S(2)}) copy-start(f32[1024]{0:T(1024)} %param.24) | copy-start | bytes 12292
  109.2 2.0 copy-start.25
  115.2 2.8 copy-start.2
  115.2 3.1 copy-start.19
  149.5 1.4 copy-start.23
  149.5 1.4 copy-start.24
  149.5 2.8 copy-start.21
  149.5 2.8 copy-start.22
  152.4 3.9 copy-start.17
  156.4 2.4 copy-start.5
  156.4 2.4 copy-start.16
  156.4 3.1 copy-start.15
  158.8 1.3 copy-start.14
  160.1 11.9 %copy-start.26 = (f32[32,4]{0,1:T(4,128)S(1)}, f32[32,4]{0,1:T(4,128)}, u32[]{:S(2)}) copy-start(f32[32,4]{0,1:T(4,128)} %param.23) | copy-start | bytes 1540
  163.5 135.9 %all-reduce.12.cloned.1.call-start = ((), (), s32[]{:S(2)}) async-start(), calls=%async_computation.2 | async-start | bytes 524288 | tf_op jit(solution)/shard_map/psum | solution.py:123
  172.0 90.3 %copy-start.3 = (bf16[256,1024]{1,0:T(8,128)(2,1)S(1)}, bf16[256,1024]{1,0:T(8,128)(2,1)}, u32[]{:S(2)}) copy-start(bf16[256,1024]{1,0:T(8,128)(2,1)} %param.27) | copy-start | bytes 1572868
  173.5 10.0 %copy-start.13 = (f32[4,4]{1,0:T(4,128)}, f32[4,4]{1,0:T(4,128)S(1)}, u32[]{:S(2)}) copy-start(f32[4,4]{1,0:T(4,128)S(1)} %copy.153) | copy-start | bytes 196
  181.6 0.6 copy-start.11
  212.3 0.6 copy-start.12
  267.7 183.0 %all-reduce.8.cloned.1.call-start = ((), (), s32[]{:S(2)}) async-start(), calls=%async_computation | async-start | bytes 524288 | tf_op jit(solution)/shard_map/psum | solution.py:141
  303.4 13.3 %slice-start = ((s8[5767168]{0:T(1024)(128)(4,1)}), s8[4194304]{0:T(1024)(128)(4,1)S(1)}, s32[]{:S(2)}) async-start(s8[5767168]{0:T(1024)(128)(4,1)} %bitcast.574), calls=%async_computation.3 | async-start | bytes 8388608
  307.8 4.4 copy-start.10
  307.8 8.9 %slice-start.1 = ((s8[5767168]{0:T(1024)(128)(4,1)}), s8[1572864]{0:T(1024)(128)(4,1)S(1)}, s32[]{:S(2)}) async-start(s8[5767168]{0:T(1024)(128)(4,1)} %bitcast.574), calls=%async_computation.4 | async-start | bytes 3145728
  323.3 127.4 %copy-start.6 = (f32[1,16,1024]{2,1,0:T(8,128)S(1)}, f32[1,16,1024]{2,1,0:T(8,128)}, u32[]{:S(2)}) copy-start(f32[1,16,1024]{2,1,0:T(8,128)} %get-tuple-element.31) | copy-start | bytes 196612
  323.3 127.4 %copy-start.7 = (f32[1,16,1024]{2,1,0:T(8,128)S(1)}, f32[1,16,1024]{2,1,0:T(8,128)}, u32[]{:S(2)}) copy-start(f32[1,16,1024]{2,1,0:T(8,128)} %get-tuple-element.32) | copy-start | bytes 196612
  323.3 127.4 %copy-start.8 = (f32[1,16,1024]{2,1,0:T(8,128)S(1)}, f32[1,16,1024]{2,1,0:T(8,128)}, u32[]{:S(2)}) copy-start(f32[1,16,1024]{2,1,0:T(8,128)} %get-tuple-element.33) | copy-start | bytes 196612
  323.3 127.4 %copy-start.9 = (f32[1,16,1024]{2,1,0:T(8,128)S(1)}, f32[1,16,1024]{2,1,0:T(8,128)}, u32[]{:S(2)}) copy-start(f32[1,16,1024]{2,1,0:T(8,128)} %get-tuple-element.34) | copy-start | bytes 196612
Sparse Core Ops, SparseCore 0:
  163.6 68.9 all-reduce.9
  267.8 31.5 all-reduce.11
  324.7 125.9 all-reduce.7
where the time goes:
time: 462 us; the launch traced here: 459 us
  waiting for transfers between devices  168 us (36%)
  local copies, waits for them, and re-layouts  149 us (32%)
  matrix products  57.1 us (12%)
  other arithmetic  48.1 us (10%)
  blocking collectives  23.4 us (5%)
  between operations  13.6 us (3%)
    psum x1, waiting for transfers between devices, layer(): mixture = lax.psum(expert_part, ('seq', 'tp'))  126 us
    gather x8, local copies, waits for them, and re-layouts, cache_part(): buckets = jnp.take(bucket_table, jnp.clip(distance, 0, table_len - 1))  92.2 us
    psum x1, waiting for transfers between devices, layer(): lax.psum(partial_value, 'tp')  30.7 us
    pmax x1, blocking collectives, merge_cache(): overall = lax.pmax(maxima, 'seq')  23.4 us
    dot_general x4, matrix products, layer(): jnp.einsum('srd,kfd->ksrf', moe_in, w_gate_up, preferred_element_type=jnp...  14.6 us
    psum x1, waiting for transfers between devices, merge_cache(): lax.psum((totals * factor, summed * factor[..., None]), 'seq')  10.9 us
  transfers between devices with their start and end apart: 3, of which 3 were waited for; matrix products, arithmetic and copies ran while one was open for 13% of the time, Pallas kernels for 0%

commit v1 on v0

--- a/solution.py
+++ b/solution.py
@@ -138,7 +138,7 @@
             jnp.bfloat16
         )
         expert_part = jnp.einsum("srf,fd->srd", hidden, w_down, preferred_element_type=jnp.float32)
-        mixture = lax.psum(expert_part, ("seq", "tp"))
+        mixture = lax.psum(lax.psum(expert_part, "tp"), "seq")
         return (mid + mixture).astype(jnp.bfloat16)
 
     outputs = [layer(start, 1) for start in range(steps_all)]

time: 462 us -> 444 us (0.961)
  waiting for transfers between devices: 168 us -> 149 us
    psum x1 -> x2, waiting for transfers between devices: 126 us -> 108 us  [layer(): mixture = lax.psum(lax.psum(expert_part, 'tp'), 'seq')]
  transfers between devices with their start and end apart: 3 -> 4, of which waited for: 3 -> 4; matrix products, arithmetic and copies ran while one was open for 13% -> 13% of each run, Pallas kernels for 0% -> 0%
where the time goes in v1:
time: 444 us; the launch traced here: 441 us
  local copies, waits for them, and re-layouts  149 us (34%)
  waiting for transfers between devices  149 us (34%)
  matrix products  57.1 us (13%)
  other arithmetic  48.1 us (11%)
  blocking collectives  23.4 us (5%)
  between operations  13.7 us (3%)
    psum x2, waiting for transfers between devices, layer(): mixture = lax.psum(lax.psum(expert_part, 'tp'), 'seq')  108 us
    gather x8, local copies, waits for them, and re-layouts, cache_part(): buckets = jnp.take(bucket_table, jnp.clip(distance, 0, table_len - 1))  92.2 us
    psum x1, waiting for transfers between devices, layer(): lax.psum(partial_value, 'tp')  30.7 us
    pmax x1, blocking collectives, merge_cache(): overall = lax.pmax(maxima, 'seq')  23.4 us
    dot_general x4, matrix products, layer(): jnp.einsum('srd,kfd->ksrf', moe_in, w_gate_up, preferred_element_type=jnp...  14.6 us
    psum x1, waiting for transfers between devices, merge_cache(): lax.psum((totals * factor, summed * factor[..., None]), 'seq')  10.9 us
    unnamed x64, local copies, waits for them, and re-layouts  9.15 us
  transfers between devices with their start and end apart: 4, of which 4 were waited for; matrix products, arithmetic and copies ran while one was open for 13% of the time, Pallas kernels for 0%

profile of v1, /device:TPU:0, one launch (start us, length us, event | category | flops | bytes accessed | tf_op | source)
XLA Modules:
  0.0 440.6 jit_solution(9112296426478459819)
XLA Ops:
  9.3 23.0 %gather_fusion.4 = s32[4096]{0:T(1024)S(1)} fusion(s32[2052]{0:T(1024)S(1)} %copy-done.1, s32[4096]{0:T(1024)S(1)} %broadcast_clamp_fusion.1), kind=kCustom, calls=%fused_computation.3.clone | custom fusion | bytes 49152 | tf_op jit(solution)/shard_map/jit(_take)/gather | solution.py:63
  32.4 23.0 %gather_fusion.6 = s32[4096]{0:T(1024)S(1)} fusion(s32[2052]{0:T(1024)S(1)} %copy-done.1, s32[4096]{0:T(1024)S(1)} %broadcast_clamp_fusion), kind=kCustom, calls=%fused_computation.4.clone | custom fusion | bytes 49152 | tf_op jit(solution)/shard_map/jit(_take)/gather | solution.py:63
  55.5 23.0 %gather_fusion.2 = s32[4096]{0:T(1024)S(1)} fusion(s32[2052]{0:T(1024)S(1)} %copy-done.1, s32[4096]{0:T(1024)S(1)} %broadcast_clamp_fusion.2), kind=kCustom, calls=%fused_computation.2.clone | custom fusion | bytes 49152 | tf_op jit(solution)/shard_map/jit(_take)/gather | solution.py:63
  79.3 23.0 %gather_fusion = s32[4096]{0:T(1024)S(1)} fusion(s32[2052]{0:T(1024)S(1)} %copy-done.1, s32[4096]{0:T(1024)S(1)} %broadcast_clamp_fusion.3), kind=kCustom, calls=%fused_computation.clone | custom fusion | bytes 49152 | tf_op jit(solution)/shard_map/jit(_take)/gather | solution.py:63
  103.0 1.8 fusion.9
  105.2 3.9 copy.134
  109.2 2.0 fusion.206
  112.2 2.0 fusion.205
  115.2 2.8 fusion.204
  126.0 23.4 %all-reduce.2 = (f32[1,16,4]{1,2,0:T(4,128)S(1)}, f32[1,16,4]{1,2,0:T(4,128)S(1)}, f32[1,16,4]{1,2,0:T(4,128)S(1)}, f32[1,16,4]{1,2,0:T(4,128)S(1)}) all-reduce(f32[1,16,4]{1,2,0:T(4,128)} %bitcast.599, f32[1,16,4]{1,2,0:T(4,128)} %bitcast.601, f32[1,16,4]{1,2,0:T(4,128)} %bitcast.598, ...), channel_id=1, replica_groups=mesh['seq'=8,'tp'=4] {'seq'}, use_global_device_ids=true, to_apply=%region_2.4 | all-reduce | flops 256 | bytes 2048 | tf_op jit(solution)/shard_map/pmax | solution.py:78
  151.0 1.3 bitcast_multiply_fusion.5
  152.4 3.9 copy.135
  156.4 2.4 fusion.63
  176.6 1.5 convolution_bitcast_fusion.15
  178.1 1.3 copy.160
  179.4 1.4 copy.186
  182.2 1.4 fusion.194
  183.6 1.4 copy.193
  185.8 1.4 fusion.193
  187.2 1.4 fusion.196
  189.8 1.3 gather_fusion.1
  191.8 1.4 convolution_bitcast_fusion.18
  193.3 1.4 copy.138
  195.9 1.3 gather_fusion.3
  199.5 1.5 reshape_squeeze.8
  202.6 1.4 fusion.192
  203.9 1.4 copy.180
  205.3 1.4 copy.187
  206.7 1.7 fusion.108
  208.4 1.7 fusion.106
  210.0 1.4 copy.171
  212.8 1.4 fusion.190
  214.2 1.4 copy.173
  215.6 1.7 fusion.110
  217.3 1.4 copy.194
  218.7 1.7 fusion.104
  220.3 1.4 fusion.189
  221.7 10.9 %all-reduce.10.cloned.1.call-done = (f32[1,16,4,64]{3,2,1,0:T(4,128)}, f32[1,16,4]{1,2,0:T(4,128)}, f32[1,16,4,64]{3,2,1,0:T(4,128)}, f32[1,16,4]{1,2,0:T(4,128)...) async-done(((f32[1,16,4,64]{3,2,1,0:T(4,128)}, f32[1,16,4]{1,2,0:T(4,128)}, f32[1,16,4,64]{3,2,1,0:T(4,128)}, ...) | async-done | bytes 66576 | tf_op jit(solution)/shard_map/psum | solution.py:80
  234.7 1.3 fusion.178
  236.0 1.3 copy.161
  240.6 1.4 copy.139
  241.9 1.3 copy.157
  243.3 1.3 copy.155
  244.6 1.5 fusion.102
  246.9 1.3 copy.164
  248.2 1.3 copy.162
  249.6 1.5 fusion.103
  251.1 1.4 convert_element_type.133
  252.5 1.3 copy.150
  253.8 1.3 copy.148
  255.2 1.5 fusion.101
  256.7 1.4 convert_element_type.121
  259.4 1.5 fusion.100
  260.9 1.4 convert_element_type.115
  262.4 1.5 convolution_bitcast_fusion.14
  263.9 1.5 convolution_bitcast_fusion.13
  265.4 1.5 convolution_bitcast_fusion.11
  268.7 30.7 %all-reduce.16.cloned.1.call-done = (f32[1,16,1024]{2,1,0:T(8,128)}, f32[1,16,1024]{2,1,0:T(8,128)}, f32[1,16,1024]{2,1,0:T(8,128)}, f32[1,16,1024]{2,1,0:T(8,128)}) async-done(((f32[1,16,1024]{2,1,0:T(8,128)}, f32[1,16,1024]{2,1,0:T(8,128)}, f32[1,16,1024]{2,1,0:T(8,128)}, f32[1,16,1024]{2,1,0:T(8,128)}), (f32[1,16,1024]{2,1,0:T(8,128)}, f32[1,16,1024]{2,1,0:T(8,128)}, f32[1,16,1024]{2,1,0:T(8,128)}, ...) | async-done | bytes 262160 | tf_op jit(solution)/shard_map/psum | solution.py:123
  303.4 4.4 fusion.95
  307.8 4.4 convolution_bitcast_fusion
  312.3 4.2 convolution_bitcast_fusion.1
  316.7 1.6 convolution_bitcast_fusion.2
  324.6 32.4 %all-reduce.14.cloned.1.call-done = (f32[1,16,1024]{2,1,0:T(8,128)}, f32[1,16,1024]{2,1,0:T(8,128)}, f32[1,16,1024]{2,1,0:T(8,128)}, f32[1,16,1024]{2,1,0:T(8,128)}) async-done(((f32[1,16,1024]{2,1,0:T(8,128)}, f32[1,16,1024]{2,1,0:T(8,128)}, f32[1,16,1024]{2,1,0:T(8,128)}, f32[1,16,1024]{2,1,0:T(8,128)}), (f32[1,16,1024]{2,1,0:T(8,128)}, f32[1,16,1024]{2,1,0:T(8,128)}, f32[1,16,1024]{2,1,0:T(8,128)}, ...) | async-done | bytes 262160 | tf_op jit(solution)/shard_map/psum | solution.py:141
  357.1 75.3 %all-reduce.12.cloned.1.call-done = (f32[1,16,1024]{2,1,0:T(8,128)}, f32[1,16,1024]{2,1,0:T(8,128)}, f32[1,16,1024]{2,1,0:T(8,128)}, f32[1,16,1024]{2,1,0:T(8,128)}) async-done(((f32[1,16,1024]{2,1,0:T(8,128)}, f32[1,16,1024]{2,1,0:T(8,128)}, f32[1,16,1024]{2,1,0:T(8,128)}, f32[1,16,1024]{2,1,0:T(8,128)}), (f32[1,16,1024]{2,1,0:T(8,128)}, f32[1,16,1024]{2,1,0:T(8,128)}, f32[1,16,1024]{2,1,0:T(8,128)}, ...) | async-done | bytes 262160 | tf_op jit(solution)/shard_map/psum | solution.py:141
  (199 shorter events, 66.0 us)
Async XLA Ops:
  6.5 313.0 %copy-start = (bf16[1408,1024]{1,0:T(8,128)(2,1)S(1)}, bf16[1408,1024]{1,0:T(8,128)(2,1)}, u32[]{:S(2)}) copy-start(bf16[1408,1024]{1,0:T(8,128)(2,1)} %param.31) | copy-start | bytes 8650756
  6.5 2.8 copy-start.1
  6.5 226.1 %all-reduce.10.cloned.1.call-start = ((), (), s32[]{:S(2)}) async-start(), calls=%async_computation | async-start | bytes 278528 | tf_op jit(solution)/shard_map/psum | solution.py:80
  55.5 23.1 %copy-start.20 = (s32[16]{0:T(128)S(1)}, s32[16]{0:T(128)}, u32[]{:S(2)}) copy-start(s32[16]{0:T(128)} %param.21) | copy-start | bytes 196
  79.3 23.8 %copy-start.4 = (bf16[4,16,1024]{2,1,0:T(8,128)(2,1)S(1)}, bf16[4,16,1024]{2,1,0:T(8,128)(2,1)}, u32[]{:S(2)}) copy-start(bf16[4,16,1024]{2,1,0:T(8,128)(2,1)} %param.18) | copy-start | bytes 393220
  79.3 23.8 %copy-start.18 = (f32[1024]{0:T(1024)S(1)}, f32[1024]{0:T(1024)}, u32[]{:S(2)}) copy-start(f32[1024]{0:T(1024)} %param.24) | copy-start | bytes 12292
  109.2 2.0 copy-start.25
  115.2 2.8 copy-start.2
  115.2 3.1 copy-start.19
  149.5 1.4 copy-start.23
  149.5 1.4 copy-start.24
  149.5 2.8 copy-start.21
  149.5 2.8 copy-start.22
  152.4 3.9 copy-start.17
  156.4 2.4 copy-start.5
  156.4 2.4 copy-start.16
  156.4 3.1 copy-start.15
  158.8 1.3 copy-start.14
  160.1 11.9 %copy-start.26 = (f32[32,4]{0,1:T(4,128)S(1)}, f32[32,4]{0,1:T(4,128)}, u32[]{:S(2)}) copy-start(f32[32,4]{0,1:T(4,128)} %param.23) | copy-start | bytes 1540
  163.5 135.9 %all-reduce.16.cloned.1.call-start = ((), (), s32[]{:S(2)}) async-start(), calls=%async_computation.3 | async-start | bytes 524288 | tf_op jit(solution)/shard_map/psum | solution.py:123
  172.0 90.3 %copy-start.3 = (bf16[256,1024]{1,0:T(8,128)(2,1)S(1)}, bf16[256,1024]{1,0:T(8,128)(2,1)}, u32[]{:S(2)}) copy-start(bf16[256,1024]{1,0:T(8,128)(2,1)} %param.27) | copy-start | bytes 1572868
  173.5 10.0 %copy-start.13 = (f32[4,4]{1,0:T(4,128)}, f32[4,4]{1,0:T(4,128)S(1)}, u32[]{:S(2)}) copy-start(f32[4,4]{1,0:T(4,128)S(1)} %copy.153) | copy-start | bytes 196
  181.6 0.6 copy-start.11
  212.3 0.6 copy-start.12
  267.7 89.3 %all-reduce.14.cloned.1.call-start = ((), (), s32[]{:S(2)}) async-start(), calls=%async_computation.2 | async-start | bytes 524288 | tf_op jit(solution)/shard_map/psum | solution.py:141
  303.4 13.3 %slice-start = ((s8[5767168]{0:T(1024)(128)(4,1)}), s8[4194304]{0:T(1024)(128)(4,1)S(1)}, s32[]{:S(2)}) async-start(s8[5767168]{0:T(1024)(128)(4,1)} %bitcast.574), calls=%async_computation.4 | async-start | bytes 8388608
  307.8 4.4 copy-start.10
  307.8 8.9 %slice-start.1 = ((s8[5767168]{0:T(1024)(128)(4,1)}), s8[1572864]{0:T(1024)(128)(4,1)S(1)}, s32[]{:S(2)}) async-start(s8[5767168]{0:T(1024)(128)(4,1)} %bitcast.574), calls=%async_computation.5 | async-start | bytes 3145728
  323.3 109.1 %copy-start.6 = (f32[1,16,1024]{2,1,0:T(8,128)S(1)}, f32[1,16,1024]{2,1,0:T(8,128)}, u32[]{:S(2)}) copy-start(f32[1,16,1024]{2,1,0:T(8,128)} %get-tuple-element.35) | copy-start | bytes 196612
  323.3 109.1 %copy-start.7 = (f32[1,16,1024]{2,1,0:T(8,128)S(1)}, f32[1,16,1024]{2,1,0:T(8,128)}, u32[]{:S(2)}) copy-start(f32[1,16,1024]{2,1,0:T(8,128)} %get-tuple-element.36) | copy-start | bytes 196612
  323.3 109.1 %copy-start.8 = (f32[1,16,1024]{2,1,0:T(8,128)S(1)}, f32[1,16,1024]{2,1,0:T(8,128)}, u32[]{:S(2)}) copy-start(f32[1,16,1024]{2,1,0:T(8,128)} %get-tuple-element.37) | copy-start | bytes 196612
  323.3 109.1 %copy-start.9 = (f32[1,16,1024]{2,1,0:T(8,128)S(1)}, f32[1,16,1024]{2,1,0:T(8,128)}, u32[]{:S(2)}) copy-start(f32[1,16,1024]{2,1,0:T(8,128)} %get-tuple-element.38) | copy-start | bytes 196612
  324.6 107.8 %all-reduce.12.cloned.1.call-start = ((), (), s32[]{:S(2)}) async-start(), calls=%async_computation.1 | async-start | bytes 524288 | tf_op jit(solution)/shard_map/psum | solution.py:141
Sparse Core Ops, SparseCore 0:
  163.6 68.9 all-reduce.9
  267.8 31.5 all-reduce.15
  324.7 32.2 all-reduce.13
  361.0 71.2 all-reduce.11
